TPU v7x, 128 devices: a whole 4x4x4 slice. The times are simulated.
128 devices in a mesh: ep: 8 (over z, core), dp: 16 (over y, x).
Axes of the slice: x: 4, y: 4, z: 4, core: 2. Of those that a mesh axis runs over, the one named last changes fastest.
Arguments:
- tokens: bfloat16 [32768, 1024], P(('ep', 'dp')), may hold values from -6 to 6
- lengths: int32 [8, 2], P('ep'), may hold values from 1 to 3072, 4096 in all within a row
- adapter_ids: int32 [8, 2], replicated, may hold values from 0 to 63
- expert_ids: int32 [32768, 8], P(('ep', 'dp')), may hold values from 0 to 31, all different within a row; in each aligned block of 256 rows (0 to 255, 256 to 511, ...) at most 96 rows name the same one
- attn_gain: bfloat16 [1024], replicated, may hold values from 0.5 to 1.5
- w_qkv: bfloat16 [1024, 2048], replicated, may hold values from -3 to 3
- w_out: bfloat16 [1024, 1024], replicated, may hold values from -0.1875 to 0.1875
- moe_gain: bfloat16 [1024], replicated, may hold values from 0.5 to 1.5
- w_router: bfloat16 [1024, 32], replicated, may hold values from -12 to 12
- w_gate_up: bfloat16 [32, 1024, 1024], P('ep'), may hold values from -0.1875 to 0.1875
- w_down: bfloat16 [32, 512, 1024], P('ep'), may hold values from -0.25 to 0.25
- adapter_in: bfloat16 [64, 1024, 64], P('dp'), may hold values from -0.1875 to 0.1875
- adapter_out: bfloat16 [64, 16, 4096], P('dp'), may hold values from -0.75 to 0.75
- adapter_expert: bfloat16 [64, 48, 512], P('dp'), may hold values from -0.75 to 0.75
Outputs:
- layer_out: bfloat16 [32768, 1024], P(('ep', 'dp'))
Inputs may be any that keep to these rules, and one draw needn't show every extreme that they name: `lengths`: each row sums to 4096. `expert_ids`: each row names 8 different experts; among the 256 rows of one device no expert is named more than 96 times.
All inputs are finite; a program needn't handle non-finite values.
Results may differ from a plain program's by a relative error of at most 0.02.
The roundings to bfloat16 on the way count: a program that leaves them out, or rounds other values in their place, can miss the bound.
Values may be sent and summed in bfloat16 or wider, within the bound.
A program may use at most 256 MiB of HBM per device.

v0:
```python
import math
import jax
import jax.numpy as jnp
from jax import lax
from jax.sharding import PartitionSpec as P

HEADS = 16
KV_HEADS = 8
HEAD = 64
CAP = 96
EPS = 1e-06
THETA = 10000.0
NEG_BIG = -1e30


def rms_norm(values_in, gain_vec):
    floats = values_in.astype(jnp.float32)
    meansq = jnp.mean(floats * floats, axis=-1, keepdims=True)
    return (floats * lax.rsqrt(meansq + EPS) * gain_vec.astype(jnp.float32)).astype(jnp.bfloat16)


def rotate(vectors, position):
    half_dim = vectors.shape[-1] // 2
    frequency = THETA ** (-jnp.arange(half_dim, dtype=jnp.float32) / half_dim)
    angles = position.astype(jnp.float32)[:, None] * frequency[None, :]
    cosine = jnp.cos(angles)[:, None, :]
    sine_val = jnp.sin(angles)[:, None, :]
    first_half = vectors[..., :half_dim]
    second_half = vectors[..., half_dim:]
    return jnp.concatenate(
        [
            first_half * cosine - second_half * sine_val,
            second_half * cosine + first_half * sine_val,
        ],
        axis=-1,
    )


def request_layout(lengths_row, first_pos, row_count):
    position = first_pos + jnp.arange(row_count, dtype=jnp.int32)
    req_ends = jnp.cumsum(lengths_row)
    starts = req_ends - lengths_row
    request = jnp.sum((position[:, None] >= req_ends[None, :]).astype(jnp.int32), axis=1)
    slot_hot = request[:, None] == jnp.arange(lengths_row.shape[0], dtype=jnp.int32)[None, :]
    req_start = jnp.sum(jnp.where(slot_hot, starts[None, :], 0), axis=1)
    return (position, req_start, slot_hot)


def low_rank(inputs, a_sel, slot_hot):
    count_r = a_sel.shape[2]
    a_cat = jnp.transpose(a_sel, (1, 0, 2)).reshape(inputs.shape[1], -1)
    coeffs = jnp.dot(inputs, a_cat, preferred_element_type=jnp.float32)
    keep_mask = jnp.repeat(slot_hot, count_r, axis=1)
    return jnp.where(keep_mask, coeffs, 0.0).astype(jnp.bfloat16)


def earlier_counts(flat_ids, n_experts):
    expert_hot = (flat_ids[:, None] == jnp.arange(n_experts, dtype=jnp.int32)[None, :]).astype(
        jnp.int32
    )
    return jnp.sum((jnp.cumsum(expert_hot, axis=0) - expert_hot) * expert_hot, axis=1)


def per_device(
    tokens,
    lengths,
    adapter_ids,
    expert_ids,
    attn_gain,
    w_qkv,
    w_out,
    moe_gain,
    w_router,
    w_gate_up,
    w_down,
    adapter_in,
    adapter_out,
    adapter_expert,
):
    n_ep = lax.axis_size("ep")
    group_idx = lax.axis_index("ep")
    row_idx = lax.axis_index("dp")
    tok_count = tokens.shape[0]
    model_width = tokens.shape[1]
    rank_r = adapter_in.shape[2] // 4
    q_width = HEADS * HEAD
    kv_width = KV_HEADS * HEAD
    qkv_width = q_width + 2 * kv_width
    group_ratio = HEADS // KV_HEADS
    ff_width = w_down.shape[1]
    exp_local = w_gate_up.shape[0]
    n_requests = lengths.shape[1]
    top_count = expert_ids.shape[1]
    position, req_start, slot_hot = request_layout(lengths[0], row_idx * tok_count, tok_count)
    group_ids = lax.dynamic_index_in_dim(adapter_ids, group_idx, 0, keepdims=False)
    all_in, all_out, all_expert = (
        lax.all_gather(adapter_in, "dp", axis=0, tiled=True),
        lax.all_gather(adapter_out, "dp", axis=0, tiled=True),
        lax.all_gather(adapter_expert, "dp", axis=0, tiled=True),
    )
    sel_in = jnp.take(all_in, group_ids, axis=0)
    sel_out = jnp.take(all_out, group_ids, axis=0)
    normed = rms_norm(tokens, attn_gain)
    z_qkv = low_rank(normed, sel_in[:, :, 0:rank_r], slot_hot)
    projected = jnp.dot(normed, w_qkv, preferred_element_type=jnp.float32)
    projected = projected + jnp.dot(
        z_qkv, sel_out[:, :, 0:qkv_width].reshape(-1, qkv_width), preferred_element_type=jnp.float32
    )
    rel_pos = position - req_start
    queries = rotate(projected[:, :q_width].reshape(tok_count, HEADS, HEAD), rel_pos).astype(
        jnp.bfloat16
    )
    keys_rot = rotate(
        projected[:, q_width : q_width + kv_width].reshape(tok_count, KV_HEADS, HEAD), rel_pos
    ).astype(jnp.bfloat16)
    keys_rot = keys_rot.reshape(tok_count, kv_width)
    values_v = projected[:, q_width + kv_width :].astype(jnp.bfloat16)
    query_grp = queries.reshape(tok_count, KV_HEADS, group_ratio, HEAD)
    score_scale = 1.0 / math.sqrt(HEAD)
    last_pos = position[tok_count - 1]
    first_start = req_start[0]
    init_state = (
        jnp.full((tok_count, KV_HEADS, group_ratio), NEG_BIG, jnp.float32),
        jnp.zeros((tok_count, KV_HEADS, group_ratio), jnp.float32),
        jnp.zeros((tok_count, KV_HEADS, group_ratio, HEAD), jnp.float32),
    )
    first_row = jnp.int32(0)
    keys_in = lax.all_gather(keys_rot, "dp", axis=0, tiled=True)
    vals_in = lax.all_gather(values_v, "dp", axis=0, tiled=True)
    rows_in = keys_in.shape[0]
    key_pos = jnp.arange(rows_in, dtype=jnp.int32)

    def compute(state):
        run_max, run_sum, run_acc = state
        scores = (
            jnp.einsum(
                "tgrd,sgd->tgrs",
                query_grp,
                keys_in.reshape(rows_in, KV_HEADS, HEAD),
                preferred_element_type=jnp.float32,
            )
            * score_scale
        )
        allowed = (key_pos[None, :] >= req_start[:, None]) & (key_pos[None, :] <= position[:, None])
        allowed = allowed[:, None, None, :]
        scores = jnp.where(allowed, scores, NEG_BIG)
        new_max = jnp.maximum(run_max, jnp.max(scores, axis=-1))
        weights = jnp.where(allowed, jnp.exp(scores - new_max[..., None]), 0.0)
        new_sum = jnp.sum(weights, axis=-1)
        mixed_vals = jnp.einsum(
            "tgrs,sgd->tgrd",
            weights.astype(jnp.bfloat16),
            vals_in.reshape(rows_in, KV_HEADS, HEAD),
            preferred_element_type=jnp.float32,
        )
        return (new_max, new_sum, mixed_vals)

    relevant = (first_row <= last_pos) & (first_row + rows_in - 1 >= first_start)
    run_max, run_sum, run_acc = lax.cond(relevant, compute, lambda state: state, init_state)
    attended = (run_acc / run_sum[..., None]).reshape(tok_count, q_width).astype(jnp.bfloat16)
    z_out = low_rank(attended, sel_in[:, :, rank_r : 2 * rank_r], slot_hot)
    residual = tokens.astype(jnp.float32) + jnp.dot(
        attended, w_out, preferred_element_type=jnp.float32
    )
    residual = residual + jnp.dot(
        z_out,
        sel_out[:, :, qkv_width : qkv_width + model_width].reshape(-1, model_width),
        preferred_element_type=jnp.float32,
    )
    residual = residual.astype(jnp.bfloat16)
    normed_two = rms_norm(residual, moe_gain)
    logits = jnp.dot(normed_two, w_router, preferred_element_type=jnp.float32)
    gate_weights = jax.nn.softmax(jnp.take_along_axis(logits, expert_ids, axis=1), axis=1)
    z_experts = low_rank(normed_two, sel_in[:, :, 2 * rank_r : 4 * rank_r], slot_hot)
    z_width = z_experts.shape[1]
    n_experts = exp_local * n_ep
    chosen = jnp.take(all_expert, adapter_ids.reshape(-1), axis=0).reshape(
        n_ep, n_requests, 3 * rank_r, ff_width
    )
    b_gate = chosen[:, :, 0:rank_r]
    b_up = chosen[:, :, rank_r : 2 * rank_r]
    blank_blk = jnp.zeros_like(b_gate)
    b_joint = jnp.concatenate(
        [jnp.concatenate([b_gate, blank_blk], axis=3), jnp.concatenate([blank_blk, b_up], axis=3)],
        axis=2,
    )
    b_joint = b_joint.reshape(n_ep, n_requests * 2 * rank_r, 2 * ff_width)
    a_down = jnp.transpose(chosen[:, :, 2 * rank_r : 3 * rank_r], (0, 3, 1, 2)).reshape(
        n_ep, ff_width, n_requests * rank_r
    )
    keep_mask = jnp.repeat(slot_hot, rank_r, axis=1)
    flat_expert = expert_ids.reshape(-1)
    earlier = earlier_counts(flat_expert, n_experts)
    slot_dest = flat_expert * CAP + earlier
    source_row = (
        jnp.full((n_experts * CAP,), tok_count, jnp.int32)
        .at[slot_dest]
        .set(jnp.arange(tok_count * top_count, dtype=jnp.int32) // top_count)
    )
    padded_x = jnp.concatenate([normed_two, jnp.zeros((1, model_width), jnp.bfloat16)])
    padded_z = jnp.concatenate([z_experts, jnp.zeros((1, z_width), jnp.bfloat16)])
    send_x = padded_x[source_row].reshape(n_ep, exp_local, CAP, model_width)
    send_z = padded_z[source_row].reshape(n_ep, exp_local, CAP, z_width)
    recv_x, recv_z = (
        lax.all_to_all(send_x, "ep", split_axis=0, concat_axis=0, tiled=True),
        lax.all_to_all(send_z, "ep", split_axis=0, concat_axis=0, tiled=True),
    )
    pre_act = jnp.einsum("jecd,edf->jecf", recv_x, w_gate_up, preferred_element_type=jnp.float32)
    pre_act = pre_act + jnp.einsum(
        "jecr,jrf->jecf", recv_z, b_joint, preferred_element_type=jnp.float32
    )
    hidden = (jax.nn.silu(pre_act[..., :ff_width]) * pre_act[..., ff_width:]).astype(jnp.bfloat16)
    expert_out = jnp.einsum(
        "jech,ehd->jecd", hidden, w_down, preferred_element_type=jnp.float32
    ).astype(jnp.bfloat16)
    down_coeff = jnp.einsum(
        "jech,jhr->jecr", hidden, a_down, preferred_element_type=jnp.float32
    ).astype(jnp.bfloat16)
    expert_out, down_coeff = (expert_out, down_coeff)
    back_out, back_coeff = (
        lax.all_to_all(expert_out, "ep", split_axis=0, concat_axis=0, tiled=True),
        lax.all_to_all(down_coeff, "ep", split_axis=0, concat_axis=0, tiled=True),
    )
    rows_out = back_out.reshape(n_experts * CAP, model_width)[slot_dest].reshape(
        tok_count, top_count, model_width
    )
    rows_coeff = back_coeff.reshape(n_experts * CAP, -1)[slot_dest].reshape(
        tok_count, top_count, -1
    )
    owner_hot = (expert_ids // exp_local)[:, :, None] == jnp.arange(n_ep, dtype=jnp.int32)[
        None, None, :
    ]
    weighted = jnp.where(owner_hot, gate_weights[:, :, None], 0.0)
    part_out = jnp.einsum(
        "tkg,tkd->tgd", weighted, rows_out.astype(jnp.float32), precision=lax.Precision.HIGHEST
    ).astype(jnp.bfloat16)
    part_coeff = jnp.einsum(
        "tkg,tkr->tgr", weighted, rows_coeff.astype(jnp.float32), precision=lax.Precision.HIGHEST
    ).astype(jnp.bfloat16)
    moe_sum = jnp.sum(part_out.astype(jnp.float32), axis=1)
    coeff_sum = jnp.sum(
        jnp.where(keep_mask[:, None, :], part_coeff.astype(jnp.float32), 0.0), axis=1
    ).astype(jnp.bfloat16)
    down_delta = jnp.dot(
        coeff_sum,
        sel_out[:, :, qkv_width + model_width : qkv_width + 2 * model_width].reshape(
            -1, model_width
        ),
        preferred_element_type=jnp.float32,
    )
    return (residual.astype(jnp.float32) + moe_sum + down_delta).astype(jnp.bfloat16)


def solution(mesh):
    return jax.shard_map(
        per_device,
        mesh=mesh,
        in_specs=(
            P(("ep", "dp"), None),
            P("ep", None),
            P(),
            P(("ep", "dp"), None),
            P(),
            P(),
            P(),
            P(),
            P(),
            P("ep", None, None),
            P("ep", None, None),
            P("dp", None, None),
            P("dp", None, None),
            P("dp", None, None),
        ),
        out_specs=P(("ep", "dp"), None),
        check_vma=False,
    )
```

profile of v0, /device:TPU:1, one launch (start us, length us, event | category | flops | bytes accessed | tf_op | source)
XLA Modules:
  0.0 616.2 jit_solution(15493466018963444724)
XLA Ops:
  17.9 65.3 %all-gather.8.cloned.1.call-done = bf16[64,16,4096]{2,1,0:T(8,128)(2,1)} async-done(((bf16[4,16,4096]{2,1,0:T(8,128)(2,1)}), bf16[64,16,4096]{2,1,0:T(8,128)(2,1)}) %all-gather.8.cloned.1.call-update) | async-done | bytes 8388624 | tf_op jit(solution)/shard_map/all_gather | solution.py:98
  88.0 67.7 %all-gather.6.cloned.1.call-done = bf16[64,1024,64]{1,2,0:T(8,128)(2,1)} async-done(((bf16[4,1024,64]{1,2,0:T(8,128)(2,1)}), bf16[64,1024,64]{1,2,0:T(8,128)(2,1)}) %all-gather.6.cloned.1.call-update) | async-done | bytes 8388624 | tf_op jit(solution)/shard_map/all_gather | solution.py:97
  179.1 15.9 %reduce-window.11 = s32[32,16,128]{2,1,0:T(8,128)S(1)} reduce-window(s32[32,16,128]{2,1,0:T(8,128)} %fusion.69, s32[]{:T(128)} %constant.130.clone.1), window={size=1x1x128 pad=0_0x0_0x127_0}, to_apply=%region_11.12 | reduce-window | flops 8323072 | bytes 524292 | tf_op jit(solution)/shard_map/reduce-window.1
  200.9 8.2 %scatter_custom_fusion = s32[3072]{0:T(1024)S(1)} fusion(s32[2048]{0:T(1024)S(1)} %bitcast.173, s32[2048]{0:T(1024)} %add_select_fusion, s32[]{:T(128)} %constant.128.clone.1), kind=kCustom, calls=%fused_computation.129 | custom fusion | bytes 12800 | tf_op jit(solution)/shard_map/scatter | solution.py:198
  213.5 12.3 %all-gather.10.cloned.1.call-done = bf16[4096,512]{0,1:T(8,128)(2,1)} async-done(((bf16[256,512]{0,1:T(8,128)(2,1)}), bf16[4096,512]{0,1:T(8,128)(2,1)}) %all-gather.10.cloned.1.call-update) | async-done | bytes 4194320 | tf_op jit(solution)/shard_map/all_gather | solution.py:128
  225.8 53.9 %all-gather.12.cloned.1.call-done = bf16[4096,512]{1,0:T(8,128)(2,1)} async-done(((bf16[256,512]{1,0:T(8,128)(2,1)}), bf16[4096,512]{1,0:T(8,128)(2,1)}) %all-gather.12.cloned.1.call-update) | async-done | bytes 4194320 | tf_op jit(solution)/shard_map/all_gather | solution.py:129
  279.7 88.2 %conditional.1 = (f32[256,8,2]{0,2,1:T(2,128)S(1)}, f32[256,8,2,64]{0,3,2,1:T(8,128)}) conditional(s32[]{:T(128)} %bitcast.12, () %tuple.13, (s32[4096]{0:T(1024)S(1)}, s32[4096]{0:T(1024)S(1)}, s32[256]{0:T(256)S(1)}, s32[256]{0:T(256)S(1)}, bf16[4096,512]{0,1:T(8,128)(2,1)}, /*index=5*/bf16[256,8,2,64]{0,3,2,1:T(8,128)(2,1)S(1)}, ...), branch_computations={%region_4.5_spmd, %region_5.8_spmd} | conditional | flops 4516212736 | bytes 224004112 | solution.py:159
  284.0 26.5 %fusion = (f32[256,8,2]{0,2,1:T(2,128)S(1)}, f32[8,4096,256,2]{2,1,3,0:T(8,128)}) fusion(pred[256,4096]{0,1:T(8,128)(4,1)} %compare_and_fusion, bf16[4096,8,64,1]{0,2,3,1:T(8,128)(2,1)} %bitcast.176, bf16[256,8,2,64]{0,3,2,1:T(8,128)(2,1)S(1)} %get-tuple-element.23), kind=kOutput, calls=%fused_computation.11 | convolution fusion | flops 2197811200 | bytes 72892416 | tf_op jit(solution)/shard_map/cond/branch_1_fun/tgrd,sgd->tgrs/dot_general | solution.py:136
  310.5 22.8 %fusion.2 = f32[256,8,2]{0,2,1:T(2,128)S(1)} fusion(f32[8,4096,256,2]{2,1,3,0:T(8,128)} %get-tuple-element.65, f32[256,8,2]{0,2,1:T(2,128)S(1)} %broadcast_maximum_fusion, pred[256,4096]{0,1:T(8,128)(4,1)} %compare_and_fusion), kind=kLoop, calls=%fused_computation.13 | loop fusion | flops 83881984 | bytes 68190208 | tf_op jit(solution)/shard_map/cond/branch_1_fun/reduce_sum | solution.py:149
  333.3 6.4 %copy.117 = bf16[4096,512]{0,1:T(8,128)(2,1)} copy(bf16[4096,512]{1,0:T(8,128)(2,1)} %get-tuple-element.63) | data formatting | bytes 8388608 | tf_op jit(solution)/shard_map
  339.7 28.1 %fusion.6 = f32[256,8,2,64]{0,3,2,1:T(8,128)} fusion(bf16[4096,8,64,1]{0,2,3,1:T(8,128)(2,1)} %bitcast.150, f32[8,4096,256,2]{2,1,3,0:T(8,128)} %get-tuple-element.65, f32[256,8,2]{0,2,1:T(2,128)S(1)} %broadcast_maximum_fusion, pred[256,4096]{0,1:T(8,128)(4,1)} %compare_and_fusion), kind=kOutput, calls=%fused_computation.17 | convolution fusion | flops 2231369728 | bytes 73416704 | tf_op jit(solution)/shard_map/cond/branch_1_fun/tgrs,sgd->tgrd/dot_general | solution.py:150
  373.1 14.0 %gather_fusion.2 = bf16[3072,1024]{1,0:T(8,128)(2,1)} fusion(bf16[257,1024]{1,0:T(8,128)(2,1)S(1)} %concatenate.32, s32[3072]{0:T(1024)S(1)} %fusion.77), kind=kCustom, calls=%fused_computation.2 | custom fusion | bytes 12595200 | tf_op jit(solution)/shard_map/gather | solution.py:202
  387.1 5.8 all-to-all-start
  397.6 9.2 %gather_fusion.3 = bf16[3072,64]{1,0:T(8,128)(2,1)S(1)} fusion(bf16[257,64]{1,0:T(8,128)(2,1)S(1)} %concatenate.33.clone, s32[3072]{0:T(1024)S(1)} %copy-done.11), kind=kCustom, calls=%fused_computation.3 | custom fusion | bytes 798720 | tf_op jit(solution)/shard_map/gather | solution.py:203
  407.9 56.4 %all-to-all-done = bf16[8,4,96,1024]{3,2,1,0:T(8,128)(2,1)} async-done(((bf16[8,4,96,1024]{3,2,1,0:T(8,128)(2,1)}), bf16[8,4,96,1024]{3,2,1,0:T(8,128)(2,1)}, u32[]{:S(2)}, u32[]{:S(2)}) %all-to-all-start) | async-done | bytes 6291488 | tf_op jit(solution)/shard_map/all_to_all | solution.py:205
  468.6 13.8 %fusion.12 = f32[4,8,96,1024]{3,2,1,0:T(8,128)} fusion(bf16[4,1024,1024]{2,1,0:T(8,128)(2,1)} %param.25, bf16[8,4,96,1024]{3,2,1,0:T(8,128)(2,1)} %all-to-all-done), kind=kOutput, calls=%fused_computation.23 | convolution fusion | flops 6442450944 | bytes 27262976 | tf_op jit(solution)/shard_map/jecd,edf->jecf/dot_general | solution.py:208
  482.4 6.7 %bitcast_add_fusion = f32[8,4,96,1024]{3,2,0,1:T(8,128)S(1)} fusion(f32[4,8,96,1024]{3,2,1,0:T(8,128)} %fusion.12, bf16[8,64,1024,1]{2,1,0,3:T(8,128)(2,1)} %bitcast.149, bf16[8,4,96,64]{2,3,1,0:T(8,128)(2,1)S(1)} %all-to-all-done.1), kind=kOutput, calls=%fused_computation.22 | convolution fusion | flops 405798912 | bytes 26607616 | tf_op jit(solution)/shard_map/jecr,jrf->jecf/dot_general | solution.py:209
  499.6 6.6 %convert_bitcast_fusion = bf16[8,4,96,1024]{3,2,0,1:T(8,128)(2,1)S(1)} fusion(bf16[8,4,96,512]{3,2,0,1:T(8,128)(2,1)} %copy-done.4, bf16[4,512,1024]{2,1,0:T(8,128)(2,1)} %param.26), kind=kOutput, calls=%fused_computation.29 | convolution fusion | flops 3224371200 | bytes 13631488 | tf_op jit(solution)/shard_map/jech,ehd->jecd/dot_general | solution.py:213
  509.6 5.2 all-to-all-start.2
  515.6 16.8 %gather_fusion.7 = f32[2048]{0:T(1024)S(1)} fusion(f32[256,32]{0,1:T(8,128)S(1)} %fusion.99, s32[2048]{0:T(1024)S(1)} %reshape.451), kind=kCustom, calls=%fused_computation.7 | custom fusion | bytes 32768 | tf_op jit(solution)/shard_map/jit(take_along_axis)/gather | solution.py:173
  533.1 6.2 %gather_fusion.6 = bf16[2048,32]{1,0:T(8,128)(2,1)S(1)} fusion(bf16[3072,32]{1,0:T(8,128)(2,1)S(1)} %bitcast.145, s32[2048]{0:T(1024)S(1)} %broadcast_clamp_fusion), kind=kCustom, calls=%fused_computation.6 | custom fusion | bytes 270336 | tf_op jit(solution)/shard_map/gather | solution.py:227
  540.6 45.3 %all-to-all-done.2 = bf16[8,4,96,1024]{3,2,1,0:T(8,128)(2,1)} async-done(((bf16[8,4,96,1024]{3,2,1,0:T(8,128)(2,1)}), bf16[8,4,96,1024]{3,2,1,0:T(8,128)(2,1)}, u32[]{:S(2)}, u32[]{:S(2)}) %all-to-all-start.2) | async-done | bytes 6291488 | tf_op jit(solution)/shard_map/all_to_all | solution.py:221
  586.0 14.8 %gather_fusion.5 = bf16[2048,1024]{1,0:T(8,128)(2,1)} fusion(bf16[3072,1024]{1,0:T(8,128)(2,1)} %bitcast.48, s32[2048]{0:T(1024)S(1)} %broadcast_clamp_fusion), kind=kCustom, calls=%fused_computation.5 | custom fusion | bytes 8396800 | tf_op jit(solution)/shard_map/gather | solution.py:224
  600.8 7.5 %convert_reduce_fusion = f32[256,1024]{1,0:T(8,128)S(1)} fusion(bf16[2048,1024]{1,0:T(8,128)(2,1)} %gather_fusion.5, f32[256,8]{1,0:T(8,128)S(1)} %copy.121, s32[256,8]{1,0:T(8,128)S(1)} %copy.118), kind=kOutput, calls=%fused_computation.25 | convolution fusion | flops 207388672 | bytes 5259264 | tf_op jit(solution)/shard_map/tkg,tkd->tgd/dot_general | solution.py:234
  (164 shorter events, 84.7 us)
Async XLA Ops:
  6.5 362.6 %copy-start = (bf16[1024,1024]{1,0:T(8,128)(2,1)S(1)}, bf16[1024,1024]{1,0:T(8,128)(2,1)}, u32[]{:S(2)}) copy-start(bf16[1024,1024]{1,0:T(8,128)(2,1)} %param.22) | copy-start | bytes 6291460
  6.5 154.0 %copy-start.2 = (bf16[256,1024]{1,0:T(8,128)(2,1)S(1)}, bf16[256,1024]{1,0:T(8,128)(2,1)}, u32[]{:S(2)}) copy-start(bf16[256,1024]{1,0:T(8,128)(2,1)} %param.16) | copy-start | bytes 1572868
  6.5 76.7 %all-gather.8.cloned.1.call-start = ((), (), s32[]{:S(2)}) async-start(), calls=%async_computation.5 | async-start | bytes 8912896 | tf_op jit(solution)/shard_map/all_gather | solution.py:98
  7.3 148.5 %all-gather.6.cloned.1.call-start = ((), (), s32[]{:S(2)}) async-start(), calls=%async_computation.4 | async-start | bytes 8912896 | tf_op jit(solution)/shard_map/all_gather | solution.py:97
  8.0 217.8 %all-gather.10.cloned.1.call-start = ((), (), s32[]{:S(2)}) async-start(), calls=%async_computation.6 | async-start | bytes 4456448 | tf_op jit(solution)/shard_map/all_gather | solution.py:128
  10.5 162.4 %copy-start.22 = (s32[256]{0:T(256)}, s32[256]{0:T(256)S(1)}, u32[]{:S(2)}) copy-start(s32[256]{0:T(256)S(1)} %iota_add_fusion) | copy-start | bytes 3076
  11.3 162.2 %copy-start.19 = (s32[256]{0:T(256)}, s32[256]{0:T(256)S(1)}, u32[]{:S(2)}) copy-start(s32[256]{0:T(256)S(1)} %select_reduce_fusion) | copy-start | bytes 3076
  12.6 152.0 %copy-start.17 = (pred[256,2]{0,1:T(4,128)(4,1)}, pred[256,2]{0,1:T(4,128)(4,1)S(1)}, u32[]{:S(2)}) copy-start(pred[256,2]{0,1:T(4,128)(4,1)S(1)} %iota_compare_fusion.7) | copy-start | bytes 1540
  17.9 156.2 %copy-start.7 = (s32[256,8]{0,1:T(8,128)S(1)}, s32[256,8]{0,1:T(8,128)}, u32[]{:S(2)}) copy-start(s32[256,8]{0,1:T(8,128)} %param.19) | copy-start | bytes 24580
  87.2 89.8 %copy-start.24 = (bf16[1024]{0:T(1024)(128)(2,1)S(1)}, bf16[1024]{0:T(1024)(128)(2,1)}, u32[]{:S(2)}) copy-start(bf16[1024]{0:T(1024)(128)(2,1)} %param.23) | copy-start | bytes 6148
  164.6 46.1 %slice-start = ((f32[256,2048]{1,0:T(8,128)}), f32[256,1024]{1,0:T(8,128)S(1)}, s32[]{:S(2)}) async-start(f32[256,2048]{1,0:T(8,128)} %convolution_add_fusion), calls=%async_computation.9 | async-start | bytes 2097152 | tf_op jit(solution)/shard_map/slice | solution.py:110
  170.4 109.3 %all-gather.12.cloned.1.call-start = ((), (), s32[]{:S(2)}) async-start(), calls=%async_computation.7 | async-start | bytes 4456448 | tf_op jit(solution)/shard_map/all_gather | solution.py:129
  172.3 221.1 %all-gather.14.cloned.1.call-start = ((), (), s32[]{:S(2)}) async-start(), calls=%async_computation.8 | async-start | bytes 3342336 | tf_op jit(solution)/shard_map/all_gather | solution.py:99
  200.0 79.6 %copy-start.20 = (s32[256]{0:T(256)S(1)}, s32[256]{0:T(256)}, u32[]{:S(2)}) copy-start(s32[256]{0:T(256)} %copy-done.19) | copy-start | bytes 3076
  200.1 79.6 %copy-start.23 = (s32[256]{0:T(256)S(1)}, s32[256]{0:T(256)}, u32[]{:S(2)}) copy-start(s32[256]{0:T(256)} %copy-done.22) | copy-start | bytes 3076
  200.9 8.2 %copy-start.14 = (s32[2048,1]{0,1:T(1,128)}, s32[2048,1]{0,1:T(1,128)S(1)}, u32[]{:S(2)}) copy-start(s32[2048,1]{0,1:T(1,128)S(1)} %compare_select_fusion) | copy-start | bytes 24580
  209.2 164.0 %copy-start.10 = (s32[3072]{0:T(1024)}, s32[3072]{0:T(1024)S(1)}, u32[]{:S(2)}) copy-start(s32[3072]{0:T(1024)S(1)} %fusion.77) | copy-start | bytes 36868
  279.7 89.5 %copy-start.3 = (bf16[256,1024]{1,0:T(8,128)(2,1)S(1)}, bf16[256,1024]{1,0:T(8,128)(2,1)}, u32[]{:S(2)}) copy-start(bf16[256,1024]{1,0:T(8,128)(2,1)} %param.16) | copy-start | bytes 1572868
  387.1 77.1 %all-to-all-start = ((bf16[8,4,96,1024]{3,2,1,0:T(8,128)(2,1)}), bf16[8,4,96,1024]{3,2,1,0:T(8,128)(2,1)}, u32[]{:S(2)}, u32[]{:S(2)}) async-start(bf16[8,4,96,1024]{3,2,1,0:T(8,128)(2,1)} %bitcast.146), calls=%async_computation | async-start | bytes 12582912 | tf_op jit(solution)/shard_map/all_to_all | solution.py:205
  464.2 18.2 %all-to-all-start.1 = ((bf16[8,4,96,64]{2,3,1,0:T(8,128)(2,1)}), bf16[8,4,96,64]{2,3,1,0:T(8,128)(2,1)S(1)}, u32[]{:S(2)}, u32[]{:S(2)}) async-start(bf16[8,4,96,64]{2,3,1,0:T(8,128)(2,1)} %copy.130), calls=%async_computation.1 | async-start | bytes 1048576 | tf_op jit(solution)/shard_map/all_to_all | solution.py:206
  494.8 14.8 %all-to-all-start.3 = ((bf16[8,4,96,32]{2,3,1,0:T(8,128)(2,1)}), bf16[8,4,96,32]{2,3,1,0:T(8,128)(2,1)S(1)}, u32[]{:S(2)}, u32[]{:S(2)}) async-start(bf16[8,4,96,32]{2,3,1,0:T(8,128)(2,1)} %fusion.45), calls=%async_computation.3 | async-start | bytes 524288 | tf_op jit(solution)/shard_map/all_to_all | solution.py:222
  509.6 76.4 %all-to-all-start.2 = ((bf16[8,4,96,1024]{3,2,1,0:T(8,128)(2,1)}), bf16[8,4,96,1024]{3,2,1,0:T(8,128)(2,1)}, u32[]{:S(2)}, u32[]{:S(2)}) async-start(bf16[8,4,96,1024]{3,2,1,0:T(8,128)(2,1)} %copy.134), calls=%async_computation.2 | async-start | bytes 12582912 | tf_op jit(solution)/shard_map/all_to_all | solution.py:221
  586.0 22.4 %copy-start.9 = (bf16[2,16,1024]{2,1,0:T(8,128)(2,1)S(1)}, bf16[2,16,1024]{2,1,0:T(8,128)(2,1)}, u32[]{:S(2)}) copy-start(bf16[2,16,1024]{2,1,0:T(8,128)(2,1)} %get-tuple-element.76) | copy-start | bytes 196612
  586.0 23.4 %copy-start.1 = (bf16[1024,1024]{1,0:T(8,128)(2,1)S(1)}, bf16[1024,1024]{1,0:T(8,128)(2,1)}, u32[]{:S(2)}) copy-start(bf16[1024,1024]{1,0:T(8,128)(2,1)} %param.22) | copy-start | bytes 6291460
  (12 other events, 49.5 us)
Sparse Core Ops, SparseCore 0:
  9.5 73.6 all-gather.7
  85.3 70.3 all-gather.5
  170.5 55.2 all-gather.9
  227.8 51.8 all-gather.11
  281.7 46.8 all-gather.13
where the time goes:
time: 623 us; the launch traced here: 616 us
  waiting for transfers between devices  303 us (49%)
  local copies, waits for them, and re-layouts  110 us (18%)
  matrix products  107 us (17%)
  other arithmetic  60.4 us (10%)
  starting transfers between devices  20.4 us (3%)
  between operations  15.4 us (2%)
    all_gather x1, waiting for transfers between devices, per_device(): lax.all_gather(adapter_in, 'dp', axis=0, tiled=True)  67.7 us
    all_gather x1, waiting for transfers between devices, per_device(): lax.all_gather(adapter_out, 'dp', axis=0, tiled=True)  65.3 us
    all_to_all x1, waiting for transfers between devices, per_device(): lax.all_to_all(send_x, 'ep', split_axis=0, concat_axis=0, tiled=True)  56.4 us
    all_gather x1, waiting for transfers between devices, per_device(): vals_in = lax.all_gather(values_v, 'dp', axis=0, tiled=True)  53.9 us
    all_to_all x1, waiting for transfers between devices, per_device(): lax.all_to_all(expert_out, 'ep', split_axis=0, concat_axis=0, tiled=True)  45.3 us
    dot_general x1, matrix products, compute(): jnp.einsum('tgrs,sgd->tgrd', weights.astype(jnp.bfloat16), vals_in.reshap...  28.1 us
    dot_general x1, matrix products, compute(): jnp.einsum('tgrd,sgd->tgrs', query_grp, keys_in.reshape(rows_in, KV_HEADS...  26.5 us
    reduce_sum x1, other arithmetic, compute(): new_sum = jnp.sum(weights, axis=-1)  22.8 us
  transfers between devices with their start and end apart: 9, of which 6 were waited for; matrix products, arithmetic and copies ran while one was open for 37% of the time, Pallas kernels for 0%

commit v1 on v0

--- a/solution.py
+++ b/solution.py
@@ -93,8 +93,28 @@
     top_count = expert_ids.shape[1]
     position, req_start, slot_hot = request_layout(lengths[0], row_idx * tok_count, tok_count)
     group_ids = lax.dynamic_index_in_dim(adapter_ids, group_idx, 0, keepdims=False)
+
+    def test_the_trails(row_axis, mat):
+        field_out = lax.axis_size(row_axis)
+        aux, t1, y1 = (field_out, lax.axis_index(row_axis), mat.shape[0])
+        parts_seen = list(map(lambda ix: (ix, (ix + 1) % aux), range(aux)))
+        buffer = list(map(lambda ix: (ix, (ix - 1) % aux), range(aux)))
+        lower = jnp.zeros((*mat.shape[:0], aux * y1, *mat.shape[1:]), mat.dtype)
+        lower = lax.dynamic_update_slice_in_dim(lower, mat, t1 * y1, axis=0)
+        met_up = big = mat
+        ii = 1
+        mid_arr = aux // 2
+        while ii < mid_arr + 1:
+            met_up = lax.ppermute(met_up, axis_name=row_axis, perm=parts_seen)
+            lower = lax.dynamic_update_slice_in_dim(lower, met_up, (t1 - ii) % aux * y1, axis=0)
+            if ii < aux - mid_arr:
+                big = lax.ppermute(big, axis_name=row_axis, perm=buffer)
+                lower = lax.dynamic_update_slice_in_dim(lower, big, (t1 + ii) % aux * y1, axis=0)
+            ii += 1
+        return lower
+
     all_in, all_out, all_expert = (
-        lax.all_gather(adapter_in, "dp", axis=0, tiled=True),
+        test_the_trails("dp", adapter_in),
         lax.all_gather(adapter_out, "dp", axis=0, tiled=True),
         lax.all_gather(adapter_expert, "dp", axis=0, tiled=True),
     )

time: 623 us -> 639 us (1.026)
  waiting for transfers between devices: 303 us -> 250 us
  starting transfers between devices: 20.4 us -> 55.9 us
  local copies, waits for them, and re-layouts: 110 us -> 139 us
    ppermute x0 -> x15, waiting for transfers between devices: none -> 81.3 us  [the longest x8 77.9 us: test_the_trails(): met_up = lax.ppermute(met_up, axis_name=row_axis, perm=parts_seen)]
    all_gather x1 -> x0, waiting for transfers between devices: 67.7 us -> none  [per_device(): lax.all_gather(adapter_in, 'dp', axis=0, tiled=True)]
    all_gather x1, waiting for transfers between devices: 65.3 us -> 0.02 us  [per_device(): lax.all_gather(adapter_out, 'dp', axis=0, tiled=True)]
    ppermute x0 -> x15, starting transfers between devices: none -> 35.1 us  [the longest x7 32.9 us: test_the_trails(): big = lax.ppermute(big, axis_name=row_axis, perm=buffer)]
    dynamic_update_slice x0 -> x16, local copies, waits for them, and re-layouts: none -> 24 us  [the longest x8 12 us: test_the_trails(): lax.dynamic_update_slice_in_dim(lower, met_up, (t1 - ii) % aux * y1, axis=0)]
  transfers between devices with their start and end apart: 9 -> 23, of which waited for: 6 -> 13; matrix products, arithmetic and copies ran while one was open for 37% -> 41% of each run, Pallas kernels for 0% -> 0%
where the time goes in v1:
time: 639 us; the launch traced here: 628 us
  waiting for transfers between devices  250 us (39%)
  local copies, waits for them, and re-layouts  139 us (22%)
  matrix products  107 us (17%)
  other arithmetic  61.2 us (10%)
  starting transfers between devices  55.9 us (9%)
  between operations  15.5 us (2%)
    ppermute x8, waiting for transfers between devices, test_the_trails(): met_up = lax.ppermute(met_up, axis_name=row_axis, perm=parts_seen)  77.9 us
    all_to_all x1, waiting for transfers between devices, per_device(): lax.all_to_all(send_x, 'ep', split_axis=0, concat_axis=0, tiled=True)  56.4 us
    all_gather x1, waiting for transfers between devices, per_device(): vals_in = lax.all_gather(values_v, 'dp', axis=0, tiled=True)  54 us
    all_to_all x1, waiting for transfers between devices, per_device(): lax.all_to_all(expert_out, 'ep', split_axis=0, concat_axis=0, tiled=True)  45.3 us
    ppermute x7, starting transfers between devices, test_the_trails(): big = lax.ppermute(big, axis_name=row_axis, perm=buffer)  32.9 us
    dot_general x1, matrix products, compute(): jnp.einsum('tgrs,sgd->tgrd', weights.astype(jnp.bfloat16), vals_in.reshap...  28.1 us
    dot_general x1, matrix products, compute(): jnp.einsum('tgrd,sgd->tgrs', query_grp, keys_in.reshape(rows_in, KV_HEADS...  26.4 us
    reduce_sum x1, other arithmetic, compute(): new_sum = jnp.sum(weights, axis=-1)  22.8 us
  transfers between devices with their start and end apart: 23, of which 13 were waited for; matrix products, arithmetic and copies ran while one was open for 41% of the time, Pallas kernels for 0%

profile of v1, /device:TPU:1, one launch (start us, length us, event | category | flops | bytes accessed | tf_op | source)
XLA Modules:
  0.0 628.2 jit_solution(8081605480300294439)
XLA Ops:
  16.8 8.1 %collective-permute-done = bf16[4,1024,64]{1,2,0:T(8,128)(2,1)S(1)} collective-permute-done((bf16[4,1024,64]{1,2,0:T(8,128)(2,1)}, bf16[4,1024,64]{1,2,0:T(8,128)(2,1)S(1)}, u32[]{:S(2)}, u32[]{:S(2)}) %collective-permute-start) | collective-permute-done | bytes 524320 | tf_op jit(solution)/shard_map/ppermute | solution.py:108
  30.6 17.7 %collective-permute-done.2 = bf16[4,1024,64]{1,2,0:T(8,128)(2,1)S(1)} collective-permute-done((bf16[4,1024,64]{1,2,0:T(8,128)(2,1)S(1)}, bf16[4,1024,64]{1,2,0:T(8,128)(2,1)S(1)}, u32[]{:S(2)}, u32[]{:S(2)}) %collective-permute-start.2) | collective-permute-done | bytes 524320 | tf_op jit(solution)/shard_map/ppermute | solution.py:108
  53.3 13.5 %collective-permute-done.4 = bf16[4,1024,64]{1,2,0:T(8,128)(2,1)S(1)} collective-permute-done((bf16[4,1024,64]{1,2,0:T(8,128)(2,1)S(1)}, bf16[4,1024,64]{1,2,0:T(8,128)(2,1)S(1)}, u32[]{:S(2)}, u32[]{:S(2)}) %collective-permute-start.4) | collective-permute-done | bytes 524320 | tf_op jit(solution)/shard_map/ppermute | solution.py:108
  76.1 18.5 %collective-permute-done.6 = bf16[4,1024,64]{1,2,0:T(8,128)(2,1)S(1)} collective-permute-done((bf16[4,1024,64]{1,2,0:T(8,128)(2,1)S(1)}, bf16[4,1024,64]{1,2,0:T(8,128)(2,1)S(1)}, u32[]{:S(2)}, u32[]{:S(2)}) %collective-permute-start.6) | collective-permute-done | bytes 524320 | tf_op jit(solution)/shard_map/ppermute | solution.py:108
  109.7 10.3 %collective-permute-done.8 = bf16[4,1024,64]{1,2,0:T(8,128)(2,1)} collective-permute-done((bf16[4,1024,64]{1,2,0:T(8,128)(2,1)S(1)}, bf16[4,1024,64]{1,2,0:T(8,128)(2,1)}, u32[]{:S(2)}, u32[]{:S(2)}) %collective-permute-start.8) | collective-permute-done | bytes 524320 | tf_op jit(solution)/shard_map/ppermute | solution.py:108
  191.2 15.9 %reduce-window.11 = s32[32,16,128]{2,1,0:T(8,128)S(1)} reduce-window(s32[32,16,128]{2,1,0:T(8,128)} %fusion.69, s32[]{:T(128)} %constant.212.clone.1), window={size=1x1x128 pad=0_0x0_0x127_0}, to_apply=%region_11.12 | reduce-window | flops 8323072 | bytes 524292 | tf_op jit(solution)/shard_map/reduce-window.1
  212.9 8.2 %scatter_custom_fusion = s32[3072]{0:T(1024)S(1)} fusion(s32[2048]{0:T(1024)S(1)} %bitcast.173, s32[2048]{0:T(1024)} %add_select_fusion, s32[]{:T(128)} %constant.210.clone.1), kind=kCustom, calls=%fused_computation.129 | custom fusion | bytes 12800 | tf_op jit(solution)/shard_map/scatter | solution.py:218
  225.5 12.1 %all-gather.7.cloned.1.call-done = bf16[4096,512]{0,1:T(8,128)(2,1)} async-done(((bf16[256,512]{0,1:T(8,128)(2,1)}), bf16[4096,512]{0,1:T(8,128)(2,1)}) %all-gather.7.cloned.1.call-update) | async-done | bytes 4194320 | tf_op jit(solution)/shard_map/all_gather | solution.py:148
  237.6 54.0 %all-gather.9.cloned.1.call-done = bf16[4096,512]{1,0:T(8,128)(2,1)} async-done(((bf16[256,512]{1,0:T(8,128)(2,1)}), bf16[4096,512]{1,0:T(8,128)(2,1)}) %all-gather.9.cloned.1.call-update) | async-done | bytes 4194320 | tf_op jit(solution)/shard_map/all_gather | solution.py:149
  291.6 88.3 %conditional.1 = (f32[256,8,2]{0,2,1:T(2,128)S(1)}, f32[256,8,2,64]{0,3,2,1:T(8,128)}) conditional(s32[]{:T(128)} %bitcast.12, () %tuple.13, (s32[4096]{0:T(1024)S(1)}, s32[4096]{0:T(1024)S(1)}, s32[256]{0:T(256)}, s32[256]{0:T(256)}, bf16[4096,512]{0,1:T(8,128)(2,1)}, /*index=5*/bf16[256,8,2,64]{0,3,2,1:T(8,128)(2,1)S(1)}, ...), branch_computations={%region_4.5_spmd, %region_5.8_spmd} | conditional | flops 4516212736 | bytes 224004112 | solution.py:179
  296.2 26.4 %fusion = (f32[256,8,2]{0,2,1:T(2,128)S(1)}, f32[8,4096,256,2]{2,1,3,0:T(8,128)}) fusion(pred[256,4096]{0,1:T(8,128)(4,1)} %compare_and_fusion, bf16[4096,8,64,1]{0,2,3,1:T(8,128)(2,1)} %bitcast.176, bf16[256,8,2,64]{0,3,2,1:T(8,128)(2,1)S(1)} %get-tuple-element.23), kind=kOutput, calls=%fused_computation.11 | convolution fusion | flops 2197811200 | bytes 72892416 | tf_op jit(solution)/shard_map/cond/branch_1_fun/tgrd,sgd->tgrs/dot_general | solution.py:156
  322.7 22.8 %fusion.2 = f32[256,8,2]{0,2,1:T(2,128)S(1)} fusion(f32[8,4096,256,2]{2,1,3,0:T(8,128)} %get-tuple-element.65, f32[256,8,2]{0,2,1:T(2,128)S(1)} %broadcast_maximum_fusion, pred[256,4096]{0,1:T(8,128)(4,1)} %compare_and_fusion), kind=kLoop, calls=%fused_computation.13 | loop fusion | flops 83881984 | bytes 68190208 | tf_op jit(solution)/shard_map/cond/branch_1_fun/reduce_sum | solution.py:169
  345.5 6.4 %copy.117 = bf16[4096,512]{0,1:T(8,128)(2,1)} copy(bf16[4096,512]{1,0:T(8,128)(2,1)} %get-tuple-element.63) | data formatting | bytes 8388608 | tf_op jit(solution)/shard_map
  351.9 28.1 %fusion.6 = f32[256,8,2,64]{0,3,2,1:T(8,128)} fusion(bf16[4096,8,64,1]{0,2,3,1:T(8,128)(2,1)} %bitcast.150, f32[8,4096,256,2]{2,1,3,0:T(8,128)} %get-tuple-element.65, f32[256,8,2]{0,2,1:T(2,128)S(1)} %broadcast_maximum_fusion, pred[256,4096]{0,1:T(8,128)(4,1)} %compare_and_fusion), kind=kOutput, calls=%fused_computation.17 | convolution fusion | flops 2231369728 | bytes 73416704 | tf_op jit(solution)/shard_map/cond/branch_1_fun/tgrs,sgd->tgrd/dot_general | solution.py:170
  385.3 14.0 %gather_fusion.2 = bf16[3072,1024]{1,0:T(8,128)(2,1)} fusion(bf16[257,1024]{1,0:T(8,128)(2,1)S(1)} %concatenate.32, s32[3072]{0:T(1024)S(1)} %fusion.77), kind=kCustom, calls=%fused_computation.2 | custom fusion | bytes 12595200 | tf_op jit(solution)/shard_map/gather | solution.py:222
  409.8 9.2 %gather_fusion.3 = bf16[3072,64]{1,0:T(8,128)(2,1)S(1)} fusion(bf16[257,64]{1,0:T(8,128)(2,1)S(1)} %concatenate.33.clone, s32[3072]{0:T(1024)S(1)} %copy-done.17), kind=kCustom, calls=%fused_computation.3 | custom fusion | bytes 798720 | tf_op jit(solution)/shard_map/gather | solution.py:223
  420.0 56.4 %all-to-all-done = bf16[8,4,96,1024]{3,2,1,0:T(8,128)(2,1)} async-done(((bf16[8,4,96,1024]{3,2,1,0:T(8,128)(2,1)}), bf16[8,4,96,1024]{3,2,1,0:T(8,128)(2,1)}, u32[]{:S(2)}, u32[]{:S(2)}) %all-to-all-start) | async-done | bytes 6291488 | tf_op jit(solution)/shard_map/all_to_all | solution.py:225
  480.7 13.8 %fusion.12 = f32[4,8,96,1024]{3,2,1,0:T(8,128)} fusion(bf16[4,1024,1024]{2,1,0:T(8,128)(2,1)} %param.25, bf16[8,4,96,1024]{3,2,1,0:T(8,128)(2,1)} %all-to-all-done), kind=kOutput, calls=%fused_computation.23 | convolution fusion | flops 6442450944 | bytes 27262976 | tf_op jit(solution)/shard_map/jecd,edf->jecf/dot_general | solution.py:228
  494.5 6.7 %bitcast_add_fusion = f32[8,4,96,1024]{3,2,0,1:T(8,128)S(1)} fusion(f32[4,8,96,1024]{3,2,1,0:T(8,128)} %fusion.12, bf16[8,64,1024,1]{2,1,0,3:T(8,128)(2,1)} %bitcast.149, bf16[8,4,96,64]{2,3,1,0:T(8,128)(2,1)S(1)} %all-to-all-done.1), kind=kOutput, calls=%fused_computation.22 | convolution fusion | flops 405798912 | bytes 26607616 | tf_op jit(solution)/shard_map/jecr,jrf->jecf/dot_general | solution.py:229
  511.7 6.6 %convert_bitcast_fusion = bf16[8,4,96,1024]{3,2,0,1:T(8,128)(2,1)S(1)} fusion(bf16[8,4,96,512]{3,2,0,1:T(8,128)(2,1)} %copy-done.4, bf16[4,512,1024]{2,1,0:T(8,128)(2,1)} %param.26), kind=kOutput, calls=%fused_computation.29 | convolution fusion | flops 3224371200 | bytes 13631488 | tf_op jit(solution)/shard_map/jech,ehd->jecd/dot_general | solution.py:233
  527.7 16.8 %gather_fusion.7 = f32[2048]{0:T(1024)S(1)} fusion(f32[256,32]{0,1:T(8,128)S(1)} %fusion.100, s32[2048]{0:T(1024)S(1)} %reshape.451), kind=kCustom, calls=%fused_computation.7 | custom fusion | bytes 32768 | tf_op jit(solution)/shard_map/jit(take_along_axis)/gather | solution.py:193
  552.7 45.3 %all-to-all-done.2 = bf16[8,4,96,1024]{3,2,1,0:T(8,128)(2,1)} async-done(((bf16[8,4,96,1024]{3,2,1,0:T(8,128)(2,1)}), bf16[8,4,96,1024]{3,2,1,0:T(8,128)(2,1)}, u32[]{:S(2)}, u32[]{:S(2)}) %all-to-all-start.2) | async-done | bytes 6291488 | tf_op jit(solution)/shard_map/all_to_all | solution.py:241
  598.0 14.8 %gather_fusion.5 = bf16[2048,1024]{1,0:T(8,128)(2,1)} fusion(bf16[3072,1024]{1,0:T(8,128)(2,1)} %bitcast.48, s32[2048]{0:T(1024)S(1)} %broadcast_clamp_fusion), kind=kCustom, calls=%fused_computation.5 | custom fusion | bytes 8396800 | tf_op jit(solution)/shard_map/gather | solution.py:244
  612.9 7.5 %convert_reduce_fusion = f32[256,1024]{1,0:T(8,128)S(1)} fusion(bf16[2048,1024]{1,0:T(8,128)(2,1)} %gather_fusion.5, f32[256,8]{1,0:T(8,128)S(1)} %copy.121, s32[256,8]{1,0:T(8,128)S(1)} %copy.118), kind=kOutput, calls=%fused_computation.25 | convolution fusion | flops 207388672 | bytes 5259264 | tf_op jit(solution)/shard_map/tkg,tkd->tgd/dot_general | solution.py:254
  (216 shorter events, 179.4 us)
Async XLA Ops:
  6.5 374.8 %copy-start = (bf16[1024,1024]{1,0:T(8,128)(2,1)S(1)}, bf16[1024,1024]{1,0:T(8,128)(2,1)}, u32[]{:S(2)}) copy-start(bf16[1024,1024]{1,0:T(8,128)(2,1)} %param.22) | copy-start | bytes 6291460
  6.5 161.4 %all-gather.5.cloned.1.call-start = ((), (), s32[]{:S(2)}) async-start(), calls=%async_computation.4 | async-start | bytes 8912896 | tf_op jit(solution)/shard_map/all_gather | solution.py:118
  7.3 230.3 %all-gather.7.cloned.1.call-start = ((), (), s32[]{:S(2)}) async-start(), calls=%async_computation.5 | async-start | bytes 4456448 | tf_op jit(solution)/shard_map/all_gather | solution.py:148
  7.3 17.6 %collective-permute-start = (bf16[4,1024,64]{1,2,0:T(8,128)(2,1)}, bf16[4,1024,64]{1,2,0:T(8,128)(2,1)S(1)}, u32[]{:S(2)}, u32[]{:S(2)}) collective-permute-start(bf16[4,1024,64]{1,2,0:T(8,128)(2,1)} %param.27), channel_id=1, source_target_pairs={{0,1},{1,2},{2,3},{3,4},{4,5},{5,6},{6,7},{7,8},{8,9},{9,10},{10,1... | collective-permute-start | bytes 1572872 | tf_op jit(solution)/shard_map/ppermute | solution.py:108
  9.4 15.6 %collective-permute-start.1 = (bf16[4,1024,64]{1,2,0:T(8,128)(2,1)}, bf16[4,1024,64]{1,2,0:T(8,128)(2,1)}, u32[]{:S(2)}, u32[]{:S(2)}) collective-permute-start(bf16[4,1024,64]{1,2,0:T(8,128)(2,1)} %param.27), channel_id=1, source_target_pairs={{0,15},{1,0},{2,1},{3,2},{4,3},{5,4},{6,5},{7,6},{8,7},{9,8},{10,9... | collective-permute-start | bytes 1572872 | tf_op jit(solution)/shard_map/ppermute | solution.py:111
  24.9 23.3 %collective-permute-start.2 = (bf16[4,1024,64]{1,2,0:T(8,128)(2,1)S(1)}, bf16[4,1024,64]{1,2,0:T(8,128)(2,1)S(1)}, u32[]{:S(2)}, u32[]{:S(2)}) collective-permute-start(bf16[4,1024,64]{1,2,0:T(8,128)(2,1)S(1)} %collective-permute-done), channel_id=1, source_target_pairs={{0,1},{1,2},{2,3},{3,4},{4,5},{5,6},{6,7},{7,8},{8,9},{9,10},{10,1... | collective-permute-start | bytes 1572872 | tf_op jit(solution)/shard_map/ppermute | solution.py:108
  25.0 23.3 %collective-permute-start.3 = (bf16[4,1024,64]{1,2,0:T(8,128)(2,1)}, bf16[4,1024,64]{1,2,0:T(8,128)(2,1)S(1)}, u32[]{:S(2)}, u32[]{:S(2)}) collective-permute-start(bf16[4,1024,64]{1,2,0:T(8,128)(2,1)} %collective-permute-done.1), channel_id=1, source_target_pairs={{0,15},{1,0},{2,1},{3,2},{4,3},{5,4},{6,5},{7,6},{8,7},{9,8},{10,9... | collective-permute-start | bytes 1572872 | tf_op jit(solution)/shard_map/ppermute | solution.py:111
  48.3 18.5 %collective-permute-start.4 = (bf16[4,1024,64]{1,2,0:T(8,128)(2,1)S(1)}, bf16[4,1024,64]{1,2,0:T(8,128)(2,1)S(1)}, u32[]{:S(2)}, u32[]{:S(2)}) collective-permute-start(bf16[4,1024,64]{1,2,0:T(8,128)(2,1)S(1)} %collective-permute-done.2), channel_id=1, source_target_pairs={{0,1},{1,2},{2,3},{3,4},{4,5},{5,6},{6,7},{7,8},{8,9},{9,10},{10,1... | collective-permute-start | bytes 1572872 | tf_op jit(solution)/shard_map/ppermute | solution.py:108
  48.4 22.2 %collective-permute-start.5 = (bf16[4,1024,64]{1,2,0:T(8,128)(2,1)S(1)}, bf16[4,1024,64]{1,2,0:T(8,128)(2,1)S(1)}, u32[]{:S(2)}, u32[]{:S(2)}) collective-permute-start(bf16[4,1024,64]{1,2,0:T(8,128)(2,1)S(1)} %collective-permute-done.3), channel_id=1, source_target_pairs={{0,15},{1,0},{2,1},{3,2},{4,3},{5,4},{6,5},{7,6},{8,7},{9,8},{10,9... | collective-permute-start | bytes 1572872 | tf_op jit(solution)/shard_map/ppermute | solution.py:111
  67.6 27.0 %collective-permute-start.6 = (bf16[4,1024,64]{1,2,0:T(8,128)(2,1)S(1)}, bf16[4,1024,64]{1,2,0:T(8,128)(2,1)S(1)}, u32[]{:S(2)}, u32[]{:S(2)}) collective-permute-start(bf16[4,1024,64]{1,2,0:T(8,128)(2,1)S(1)} %collective-permute-done.4), channel_id=1, source_target_pairs={{0,1},{1,2},{2,3},{3,4},{4,5},{5,6},{6,7},{7,8},{8,9},{9,10},{10,1... | collective-permute-start | bytes 1572872 | tf_op jit(solution)/shard_map/ppermute | solution.py:108
  70.6 29.4 %collective-permute-start.7 = (bf16[4,1024,64]{1,2,0:T(8,128)(2,1)S(1)}, bf16[4,1024,64]{1,2,0:T(8,128)(2,1)}, u32[]{:S(2)}, u32[]{:S(2)}) collective-permute-start(bf16[4,1024,64]{1,2,0:T(8,128)(2,1)S(1)} %collective-permute-done.5), channel_id=1, source_target_pairs={{0,15},{1,0},{2,1},{3,2},{4,3},{5,4},{6,5},{7,6},{8,7},{9,8},{10,9... | collective-permute-start | bytes 1572872 | tf_op jit(solution)/shard_map/ppermute | solution.py:111
  94.6 25.3 %collective-permute-start.8 = (bf16[4,1024,64]{1,2,0:T(8,128)(2,1)S(1)}, bf16[4,1024,64]{1,2,0:T(8,128)(2,1)}, u32[]{:S(2)}, u32[]{:S(2)}) collective-permute-start(bf16[4,1024,64]{1,2,0:T(8,128)(2,1)S(1)} %collective-permute-done.6), channel_id=1, source_target_pairs={{0,1},{1,2},{2,3},{3,4},{4,5},{5,6},{6,7},{7,8},{8,9},{9,10},{10,1... | collective-permute-start | bytes 1572872 | tf_op jit(solution)/shard_map/ppermute | solution.py:108
  99.9 24.9 %collective-permute-start.9 = (bf16[4,1024,64]{1,2,0:T(8,128)(2,1)}, bf16[4,1024,64]{1,2,0:T(8,128)(2,1)}, u32[]{:S(2)}, u32[]{:S(2)}) collective-permute-start(bf16[4,1024,64]{1,2,0:T(8,128)(2,1)} %collective-permute-done.7), channel_id=1, source_target_pairs={{0,15},{1,0},{2,1},{3,2},{4,3},{5,4},{6,5},{7,6},{8,7},{9,8},{10,9... | collective-permute-start | bytes 1572872 | tf_op jit(solution)/shard_map/ppermute | solution.py:111
  120.0 14.9 %collective-permute-start.10 = (bf16[4,1024,64]{1,2,0:T(8,128)(2,1)}, bf16[4,1024,64]{1,2,0:T(8,128)(2,1)}, u32[]{:S(2)}, u32[]{:S(2)}) collective-permute-start(bf16[4,1024,64]{1,2,0:T(8,128)(2,1)} %collective-permute-done.8), channel_id=1, source_target_pairs={{0,1},{1,2},{2,3},{3,4},{4,5},{5,6},{6,7},{7,8},{8,9},{9,10},{10,1... | collective-permute-start | bytes 1572872 | tf_op jit(solution)/shard_map/ppermute | solution.py:108
  124.9 17.5 %collective-permute-start.11 = (bf16[4,1024,64]{1,2,0:T(8,128)(2,1)}, bf16[4,1024,64]{1,2,0:T(8,128)(2,1)S(1)}, u32[]{:S(2)}, u32[]{:S(2)}) collective-permute-start(bf16[4,1024,64]{1,2,0:T(8,128)(2,1)} %collective-permute-done.9), channel_id=1, source_target_pairs={{0,15},{1,0},{2,1},{3,2},{4,3},{5,4},{6,5},{7,6},{8,7},{9,8},{10,9... | collective-permute-start | bytes 1572872 | tf_op jit(solution)/shard_map/ppermute | solution.py:111
  134.8 14.3 %collective-permute-start.12 = (bf16[4,1024,64]{1,2,0:T(8,128)(2,1)}, bf16[4,1024,64]{1,2,0:T(8,128)(2,1)S(1)}, u32[]{:S(2)}, u32[]{:S(2)}) collective-permute-start(bf16[4,1024,64]{1,2,0:T(8,128)(2,1)} %collective-permute-done.10), channel_id=1, source_target_pairs={{0,1},{1,2},{2,3},{3,4},{4,5},{5,6},{6,7},{7,8},{8,9},{9,10},{10,1... | collective-permute-start | bytes 1572872 | tf_op jit(solution)/shard_map/ppermute | solution.py:108
  142.4 12.7 %collective-permute-start.13 = (bf16[4,1024,64]{1,2,0:T(8,128)(2,1)S(1)}, bf16[4,1024,64]{1,2,0:T(8,128)(2,1)S(1)}, u32[]{:S(2)}, u32[]{:S(2)}) collective-permute-start(bf16[4,1024,64]{1,2,0:T(8,128)(2,1)S(1)} %collective-permute-done.11), channel_id=1, source_target_pairs={{0,15},{1,0},{2,1},{3,2},{4,3},{5,4},{6,5},{7,6},{8,7},{9,8},{10,9... | collective-permute-start | bytes 1572872 | tf_op jit(solution)/shard_map/ppermute | solution.py:111
  149.1 13.1 %collective-permute-start.14 = (bf16[4,1024,64]{1,2,0:T(8,128)(2,1)S(1)}, bf16[4,1024,64]{1,2,0:T(8,128)(2,1)S(1)}, u32[]{:S(2)}, u32[]{:S(2)}) collective-permute-start(bf16[4,1024,64]{1,2,0:T(8,128)(2,1)S(1)} %collective-permute-done.12), channel_id=1, source_target_pairs={{0,1},{1,2},{2,3},{3,4},{4,5},{5,6},{6,7},{7,8},{8,9},{9,10},{10,1... | collective-permute-start | bytes 1572872 | tf_op jit(solution)/shard_map/ppermute | solution.py:108
  182.5 109.1 %all-gather.9.cloned.1.call-start = ((), (), s32[]{:S(2)}) async-start(), calls=%async_computation.6 | async-start | bytes 4456448 | tf_op jit(solution)/shard_map/all_gather | solution.py:149
  184.4 221.0 %all-gather.11.cloned.1.call-start = ((), (), s32[]{:S(2)}) async-start(), calls=%async_computation.7 | async-start | bytes 3342336 | tf_op jit(solution)/shard_map/all_gather | solution.py:119
  399.3 77.1 %all-to-all-start = ((bf16[8,4,96,1024]{3,2,1,0:T(8,128)(2,1)}), bf16[8,4,96,1024]{3,2,1,0:T(8,128)(2,1)}, u32[]{:S(2)}, u32[]{:S(2)}) async-start(bf16[8,4,96,1024]{3,2,1,0:T(8,128)(2,1)} %bitcast.146), calls=%async_computation | async-start | bytes 12582912 | tf_op jit(solution)/shard_map/all_to_all | solution.py:225
  476.3 18.2 %all-to-all-start.1 = ((bf16[8,4,96,64]{2,3,1,0:T(8,128)(2,1)}), bf16[8,4,96,64]{2,3,1,0:T(8,128)(2,1)S(1)}, u32[]{:S(2)}, u32[]{:S(2)}) async-start(bf16[8,4,96,64]{2,3,1,0:T(8,128)(2,1)} %copy.130), calls=%async_computation.1 | async-start | bytes 1048576 | tf_op jit(solution)/shard_map/all_to_all | solution.py:226
  506.9 14.8 %all-to-all-start.3 = ((bf16[8,4,96,32]{2,3,1,0:T(8,128)(2,1)}), bf16[8,4,96,32]{2,3,1,0:T(8,128)(2,1)S(1)}, u32[]{:S(2)}, u32[]{:S(2)}) async-start(bf16[8,4,96,32]{2,3,1,0:T(8,128)(2,1)} %fusion.45), calls=%async_computation.3 | async-start | bytes 524288 | tf_op jit(solution)/shard_map/all_to_all | solution.py:242
  521.6 76.4 %all-to-all-start.2 = ((bf16[8,4,96,1024]{3,2,1,0:T(8,128)(2,1)}), bf16[8,4,96,1024]{3,2,1,0:T(8,128)(2,1)}, u32[]{:S(2)}, u32[]{:S(2)}) async-start(bf16[8,4,96,1024]{3,2,1,0:T(8,128)(2,1)} %copy.134), calls=%async_computation.2 | async-start | bytes 12582912 | tf_op jit(solution)/shard_map/all_to_all | solution.py:241
  (30 other events, 1316.8 us)
Sparse Core Ops, SparseCore 0:
  9.5 109.1 all-gather.4
  182.7 54.8 all-gather.6
  239.7 51.8 all-gather.8
  293.6 46.8 all-gather.10
